TPU v7x, 32 devices: a whole 2x2x4 slice. The times are simulated.
32 devices in a mesh: chan: 2 (over x), srow: 4 (over y, core), scol: 4 (over z).
Axes of the slice: x: 2, y: 2, z: 4, core: 2. Of those that a mesh axis runs over, the one named last changes fastest.
Arguments:
- vis: bfloat16 [2, 2, 512, 512], P('chan', None, 'srow', 'scol'), may hold values from -4 to 4
- model: bfloat16 [2, 64, 2, 512, 512], P('chan', None, None, 'srow', 'scol'), may hold values from -1 to 1, as said below
- flags: int32 [2, 32, 32], P('chan', 'srow', 'scol'), may hold values 0 or 1
- gains: float32 [2, 64, 2, 512], P('chan', None, None, ('srow', 'scol')), may hold values from -3 to 3
- consensus: float32 [64, 1, 2, 512], P(None, None, None, ('srow', 'scol')), may hold values from -3 to 3
- dual: float32 [2, 64, 2, 512], P('chan', None, None, ('srow', 'scol')), may hold values from -2 to 2
- rho: float32 [8], replicated, may hold values from 0.5 to 8
- cluster: int32 [64], replicated, may hold values from 0 to 7
Outputs:
- gains_out: float32 [2, 64, 2, 512], P('chan', None, None, ('srow', 'scol'))
- consensus_out: float32 [64, 1, 2, 512], P(None, None, None, ('srow', 'scol'))
- dual_out: float32 [2, 64, 2, 512], P('chan', None, None, ('srow', 'scol'))
Inputs may be any that keep to these rules, and one draw needn't show every extreme that they name: `model`: entries of about 1 / sqrt(512) in size.
All inputs are finite; a program needn't handle non-finite values. No bound on the sum of `flags` on one device may be relied on, other than what follows from the above.
Results may differ from a plain program's by a relative error of at most 0.0003.
Values sent between devices are 32-bit elements; how exact they have to be, the bound alone decides.
No kernel may reach another device: no remote copies, remote signals or barrier semaphores. Data moves between devices by JAX's collectives and lax.ppermute only.
A program may use at most 64 MiB of HBM per device.

v0:
```python
import math
import jax
import jax.numpy as jnp
from jax import lax
from jax.sharding import PartitionSpec as P

STATIONS = 512
TILE = 16
ITERS = 4
EPS = 1e-05
STEP = 0.5


def basis_table(groups, order):
    xval = (jnp.arange(groups, dtype=jnp.float32) + 0.5) / groups
    columns = [
        math.comb(order - 1, b) * xval**b * (1.0 - xval) ** (order - 1 - b) for b in range(order)
    ]
    return jnp.stack(columns, axis=1)


def local_terms(vis_block, model_block, weight, g_row, g_col):
    m_real = model_block[:, 0].astype(jnp.float32)
    m_imag = model_block[:, 1].astype(jnp.float32)
    c_real = g_col[:, 0][:, None, :]
    c_imag = g_col[:, 1][:, None, :]
    z_real = m_real * c_real + m_imag * c_imag
    z_imag = m_imag * c_real - m_real * c_imag
    r_real = g_row[:, 0][:, :, None]
    r_imag = g_row[:, 1][:, :, None]
    pred_real = jnp.sum(r_real * z_real - r_imag * z_imag, axis=0)
    pred_imag = jnp.sum(r_real * z_imag + r_imag * z_real, axis=0)
    res_real = vis_block[0].astype(jnp.float32) - pred_real
    res_imag = vis_block[1].astype(jnp.float32) - pred_imag
    w_real = weight * res_real
    w_imag = weight * res_imag
    power = jnp.sum(w_real * res_real + w_imag * res_imag)
    a_term = jnp.sum(weight[None] * (z_real * z_real + z_imag * z_imag), axis=-1)
    cross_real = jnp.sum(z_real * w_real[None] + z_imag * w_imag[None], axis=-1)
    cross_imag = jnp.sum(z_real * w_imag[None] - z_imag * w_real[None], axis=-1)
    return (power, a_term, jnp.stack([cross_real, cross_imag], axis=-2))


def solve(cross, a_term, g_now, target, rho_eff):
    denom = a_term + rho_eff[:, None]
    fresh = (cross + a_term[..., None, :] * g_now + rho_eff[:, None, None] * target) / denom[
        ..., None, :
    ]
    return g_now + STEP * (fresh - g_now)


def gram_solve(table, rhs):
    gram = jnp.dot(table.T, table, precision=lax.Precision.HIGHEST)
    factor = jnp.linalg.cholesky(gram)
    order = rhs.shape[1]
    flat = jnp.moveaxis(rhs, 1, 0).reshape(order, -1)
    sol = jax.scipy.linalg.cho_solve((factor, True), flat)
    return jnp.moveaxis(sol.reshape((order, rhs.shape[0]) + rhs.shape[2:]), 0, 1)


def sweep_terms(vis_block, model_block, weight, g_row, own_gains, rho_dir, groups):
    g_col = lax.all_gather(own_gains, "srow", axis=2, tiled=True)
    power, a_term, cross = local_terms(vis_block, model_block, weight, g_row, g_col)
    total = lax.psum(power, ("chan", "srow", "scol"))
    rho_eff = rho_dir * (total / (groups * STATIONS * STATIONS) + EPS)
    return (a_term, cross, rho_eff)


def shards(vis, model, flags, gains, consensus, dual, rho, cluster):
    groups = lax.axis_size("chan")
    order = consensus.shape[1]
    table = basis_table(groups, order)
    brow = lax.dynamic_index_in_dim(table, lax.axis_index("chan"), 0, keepdims=False)
    matches = cluster[:, None] == jnp.arange(rho.shape[0], dtype=jnp.int32)[None, :]
    rho_dir = jnp.sum(jnp.where(matches, rho[None, :], 0.0), axis=1)
    fl = flags[0].astype(jnp.float32)
    weight = jnp.repeat(jnp.repeat(fl, TILE, axis=0), TILE, axis=1)
    vis_block = vis[0]
    model_block = model[0]
    dual_own = dual[0]
    target = jnp.einsum("b,kbcp->kcp", brow, consensus, precision=lax.Precision.HIGHEST) - dual_own
    g = gains[0]
    for step in range(ITERS):
        g_row = lax.all_gather(g, "scol", axis=2, tiled=True)
        a_term, cross, rho_eff = sweep_terms(
            vis_block, model_block, weight, g_row, g, rho_dir, groups
        )
        a_own, cross_own = (
            lax.psum_scatter(a_term[:, None, :], "scol", scatter_dimension=2, tiled=True),
            lax.psum_scatter(cross, "scol", scatter_dimension=2, tiled=True),
        )
        g = solve(cross_own, a_own[:, 0, :], g, target, rho_eff)
    local = brow[None, :, None, None] * (g + dual_own)[:, None, :, :]
    sums = lax.psum(local, "chan")
    coeffs = gram_solve(table, sums)
    dual_new = (
        dual_own + g - jnp.einsum("b,kbcp->kcp", brow, coeffs, precision=lax.Precision.HIGHEST)
    )
    return (g[None], coeffs, dual_new[None])


def solution(mesh):
    placed = (
        P("chan", None, "srow", "scol"),
        P("chan", None, None, "srow", "scol"),
        P("chan", "srow", "scol"),
        P("chan", None, None, ("srow", "scol")),
        P(None, None, None, ("srow", "scol")),
        P("chan", None, None, ("srow", "scol")),
        P(),
        P(),
    )
    return jax.shard_map(
        shards,
        mesh=mesh,
        in_specs=placed,
        out_specs=(
            P("chan", None, None, ("srow", "scol")),
            P(None, None, None, ("srow", "scol")),
            P("chan", None, None, ("srow", "scol")),
        ),
        check_vma=False,
    )
```

profile of v0, /device:TPU:0, one launch (start us, length us, event | category | flops | bytes accessed | tf_op | source)
XLA Modules:
  0.0 436.5 jit_solution(12146551925661814514)
XLA Ops:
  7.2 15.3 %all-gather.1 = f32[1,64,2,128]{1,3,2,0:T(8,128)S(1)} all-gather(f32[1,64,2,32]{1,3,2,0:T(8,128)} %param.11), channel_id=3, replica_groups=mesh['chan'=2,'srow'=4,'scol'=4] {'scol'}, dimensions={3}, use_global_device_ids=true | all-gather | bytes 81920 | tf_op jit(solution)/shard_map/all_gather | solution.py:84
  22.5 5.6 %all-gather = f32[1,64,2,128]{1,3,2,0:T(8,128)S(1)} all-gather(f32[1,64,2,32]{1,3,2,0:T(8,128)} %param.11), channel_id=2, replica_groups=mesh['chan'=2,'srow'=4,'scol'=4] {'srow'}, dimensions={3}, use_global_device_ids=true | all-gather | bytes 81920 | tf_op jit(solution)/shard_map/all_gather | solution.py:62
  28.5 0.7 convert_bitcast_fusion
  29.6 6.2 %subtract_reduce_fusion.7 = (f32[128,128]{1,0:T(8,128)S(1)}, f32[128,128]{1,0:T(8,128)S(1)}) fusion(f32[64,128]{1,0:T(8,128)S(1)} %copy.125, f32[64,128]{1,0:T(8,128)S(1)} %copy.124, f32[64,128]{1,0:T(8,128)S(1)} %copy.122, f32[64,128]{1,0:T(8,128)S(1)} %copy.121, bf16[64,2,128,128]{3,2,1,0:T(8,128)(2,1)} %bitcast.195), kind=kLoop, calls=%fused_computation.43 | loop fusion | flops 16744448 | bytes 4456448 | tf_op jit(solution)/shard_map/reduce_sum | solution.py:31
  35.8 0.6 add_reduce_fusion.11
  36.4 4.1 add_reduce_fusion.6
  40.6 0.7 copy.130
  41.4 0.8 copy.128
  44.0 41.0 %psum.35 = f32[]{:T(128)} all-reduce(f32[]{:T(128)} %get-tuple-element.47), channel_id=1, replica_groups=mesh['chan'=2,'srow'=4,'scol'=4] {'chan','srow','scol'}, use_global_device_ids=true, to_apply=%region_9.10 | all-reduce | flops 1 | bytes 8 | tf_op jit(solution)/shard_map/psum | solution.py:64
  87.2 0.7 broadcast_add_fusion.3
  87.9 9.0 %all-reduce.9.cloned.1.call-done = f32[64,2,128]{0,1,2:T(2,128)} async-done(((f32[64,2,128]{0,1,2:T(2,128)}), f32[64,2,128]{0,1,2:T(2,128)}) %all-reduce.9.cloned.1.call-update) | async-done | bytes 65552
  96.9 0.9 bitcast_add_fusion.1
  97.8 13.5 %all_gather.27 = f32[64,2,128]{0,1,2:T(2,128)S(1)} all-gather(f32[64,2,32]{0,1,2:T(2,128)S(1)} %get-tuple-element.45), channel_id=1, replica_groups=mesh['chan'=2,'srow'=4,'scol'=4] {'scol'}, dimensions={2}, use_global_device_ids=true | all-gather | bytes 81920 | tf_op jit(solution)/shard_map/all_gather | solution.py:84
  111.3 5.4 %all_gather.26 = f32[64,2,128]{0,1,2:T(2,128)S(1)} all-gather(f32[64,2,32]{0,1,2:T(2,128)S(1)} %get-tuple-element.45), channel_id=1, replica_groups=mesh['chan'=2,'srow'=4,'scol'=4] {'srow'}, dimensions={2}, use_global_device_ids=true | all-gather | bytes 81920 | tf_op jit(solution)/shard_map/all_gather | solution.py:62
  117.3 6.2 %subtract_reduce_fusion.5 = (f32[128,128]{1,0:T(8,128)S(1)}, f32[128,128]{1,0:T(8,128)S(1)}) fusion(f32[64,128]{1,0:T(8,128)S(1)} %copy.136, f32[64,128]{1,0:T(8,128)S(1)} %copy.135, f32[64,128]{1,0:T(8,128)S(1)} %copy.134, f32[64,128]{1,0:T(8,128)S(1)} %copy.133, bf16[64,2,128,128]{3,2,1,0:T(8,128)(2,1)} %bitcast.196), kind=kLoop, calls=%fused_computation.38 | loop fusion | flops 16744448 | bytes 4456448 | tf_op jit(solution)/shard_map/reduce_sum | solution.py:31
  123.5 0.6 add_reduce_fusion.10
  124.1 4.1 add_reduce_fusion.4
  128.2 0.7 copy.140
  129.0 39.0 %psum.36 = f32[]{:T(128)} all-reduce(f32[]{:T(128)} %get-tuple-element.42), channel_id=1, replica_groups=mesh['chan'=2,'srow'=4,'scol'=4] {'chan','srow','scol'}, use_global_device_ids=true, to_apply=%region_18.19 | all-reduce | flops 1 | bytes 8 | tf_op jit(solution)/shard_map/psum | solution.py:64
  168.7 0.8 copy.139
  169.5 0.7 broadcast_add_fusion.2
  170.3 33.9 %all-reduce.11.cloned.1.call-done = f32[64,2,128]{0,1,2:T(2,128)} async-done(((f32[64,2,128]{0,1,2:T(2,128)}), f32[64,2,128]{0,1,2:T(2,128)}) %all-reduce.11.cloned.1.call-update) | async-done | bytes 65552
  204.2 0.8 multiply_add_fusion.2
  205.0 13.5 %all_gather.29 = f32[64,2,128]{0,1,2:T(2,128)S(1)} all-gather(f32[64,2,32]{0,1,2:T(2,128)S(1)} %multiply_add_fusion.2), channel_id=1, replica_groups=mesh['chan'=2,'srow'=4,'scol'=4] {'scol'}, dimensions={2}, use_global_device_ids=true | all-gather | bytes 81920 | tf_op jit(solution)/shard_map/all_gather | solution.py:84
  218.5 5.6 %all_gather.28 = f32[64,2,128]{0,1,2:T(2,128)S(1)} all-gather(f32[64,2,32]{0,1,2:T(2,128)S(1)} %multiply_add_fusion.2), channel_id=1, replica_groups=mesh['chan'=2,'srow'=4,'scol'=4] {'srow'}, dimensions={2}, use_global_device_ids=true | all-gather | bytes 81920 | tf_op jit(solution)/shard_map/all_gather | solution.py:62
  224.7 6.2 %subtract_reduce_fusion.3 = (f32[128,128]{1,0:T(8,128)S(1)}, f32[128,128]{1,0:T(8,128)S(1)}) fusion(f32[64,128]{1,0:T(8,128)S(1)} %copy.144, f32[64,128]{1,0:T(8,128)S(1)} %copy.143, f32[64,128]{1,0:T(8,128)S(1)} %copy.142, f32[64,128]{1,0:T(8,128)S(1)} %copy.141, bf16[64,2,128,128]{3,2,1,0:T(8,128)(2,1)} %bitcast.197), kind=kLoop, calls=%fused_computation.33 | loop fusion | flops 16744448 | bytes 4456448 | tf_op jit(solution)/shard_map/reduce_sum | solution.py:31
  230.9 0.6 add_reduce_fusion.9
  231.5 4.1 add_reduce_fusion.2
  235.6 0.7 copy.148
  236.4 38.9 %psum.37 = f32[]{:T(128)} all-reduce(f32[]{:T(128)} %get-tuple-element.39), channel_id=1, replica_groups=mesh['chan'=2,'srow'=4,'scol'=4] {'chan','srow','scol'}, use_global_device_ids=true, to_apply=%region_27.28 | all-reduce | flops 1 | bytes 8 | tf_op jit(solution)/shard_map/psum | solution.py:64
  276.0 0.8 copy.147
  276.9 0.7 broadcast_add_fusion.1
  277.6 33.9 %all-reduce.13.cloned.1.call-done = f32[64,2,128]{0,1,2:T(2,128)} async-done(((f32[64,2,128]{0,1,2:T(2,128)}), f32[64,2,128]{0,1,2:T(2,128)}) %all-reduce.13.cloned.1.call-update) | async-done | bytes 65552
  311.5 0.8 multiply_add_fusion.1
  312.3 13.6 %all_gather.31 = f32[64,2,128]{0,1,2:T(2,128)S(1)} all-gather(f32[64,2,32]{0,1,2:T(2,128)S(1)} %multiply_add_fusion.1), channel_id=1, replica_groups=mesh['chan'=2,'srow'=4,'scol'=4] {'scol'}, dimensions={2}, use_global_device_ids=true | all-gather | bytes 81920 | tf_op jit(solution)/shard_map/all_gather | solution.py:84
  325.9 5.4 %all_gather.30 = f32[64,2,128]{0,1,2:T(2,128)S(1)} all-gather(f32[64,2,32]{0,1,2:T(2,128)S(1)} %multiply_add_fusion.1), channel_id=1, replica_groups=mesh['chan'=2,'srow'=4,'scol'=4] {'srow'}, dimensions={2}, use_global_device_ids=true | all-gather | bytes 81920 | tf_op jit(solution)/shard_map/all_gather | solution.py:62
  331.8 6.2 %subtract_reduce_fusion.1 = (f32[128,128]{1,0:T(8,128)S(1)}, f32[128,128]{1,0:T(8,128)S(1)}) fusion(f32[64,128]{1,0:T(8,128)S(1)} %copy.152, f32[64,128]{1,0:T(8,128)S(1)} %copy.151, f32[64,128]{1,0:T(8,128)S(1)} %copy.150, f32[64,128]{1,0:T(8,128)S(1)} %copy.149, bf16[64,2,128,128]{3,2,1,0:T(8,128)(2,1)} %bitcast.198), kind=kLoop, calls=%fused_computation.28 | loop fusion | flops 16744448 | bytes 4456448 | tf_op jit(solution)/shard_map/reduce_sum | solution.py:31
  338.0 0.6 add_reduce_fusion.8
  338.6 4.1 add_reduce_fusion
  342.8 0.7 copy.156
  343.6 38.9 %psum.38 = f32[]{:T(128)} all-reduce(f32[]{:T(128)} %get-tuple-element.36), channel_id=1, replica_groups=mesh['chan'=2,'srow'=4,'scol'=4] {'chan','srow','scol'}, use_global_device_ids=true, to_apply=%region_36.37 | all-reduce | flops 1 | bytes 8 | tf_op jit(solution)/shard_map/psum | solution.py:64
  383.2 0.8 copy.155
  384.0 0.7 broadcast_add_fusion
  384.7 33.9 %all-reduce.15.cloned.1.call-done = f32[64,2,128]{0,1,2:T(2,128)} async-done(((f32[64,2,128]{0,1,2:T(2,128)}), f32[64,2,128]{0,1,2:T(2,128)}) %all-reduce.15.cloned.1.call-update) | async-done | bytes 65552
  418.6 0.8 fusion.21
  419.5 0.6 copy.157
  420.1 8.3 %psum.39 = f32[64,1,2,32]{0,2,3,1:T(2,128)S(1)} all-reduce(f32[64,1,2,32]{0,2,3,1:T(2,128)S(1)} %get-tuple-element.34), channel_id=1, replica_groups=mesh['chan'=2,'srow'=4,'scol'=4] {'chan'}, use_global_device_ids=true, to_apply=%region_37.38 | all-reduce | flops 4096 | bytes 32768 | tf_op jit(solution)/shard_map/psum | solution.py:94
  428.4 0.6 copy.158
  (84 shorter events, 4.8 us)
Async XLA Ops:
  7.2 28.6 %copy-start.4 = (bf16[1,2,128,128]{3,2,1,0:T(8,128)(2,1)S(1)}, bf16[1,2,128,128]{3,2,1,0:T(8,128)(2,1)}, u32[]{:S(2)}) copy-start(bf16[1,2,128,128]{3,2,1,0:T(8,128)(2,1)} %param.8) | copy-start | bytes 196612
  7.2 80.0 %reduce-scatter.5.cloned.1.call-start = ((), (), s32[]{:S(2)}) async-start(), calls=%async_computation.4 | async-start | bytes 81920 | tf_op jit(solution)/shard_map/reduce_scatter | solution.py:89
  29.5 6.9 %copy-start = (bf16[1,64,2,128,128]{4,3,2,1,0:T(8,128)(2,1)S(1)}, bf16[1,64,2,128,128]{4,3,2,1,0:T(8,128)(2,1)}, u32[]{:S(2)}) copy-start(bf16[1,64,2,128,128]{4,3,2,1,0:T(8,128)(2,1)} %param.9) | copy-start | bytes 12582916
  29.5 13.3 %copy-start.10 = (u32[32]{0:T(128)S(1)}, u32[32]{0:T(128)}, u32[]{:S(2)}) copy-start(u32[32]{0:T(128)} %constant.53) | copy-start | bytes 388
  29.5 56.8 %copy-start.8 = (f32[8]{0:T(128)S(1)}, f32[8]{0:T(128)}, u32[]{:S(2)}) copy-start(f32[8]{0:T(128)} %param.14) | copy-start | bytes 100
  29.5 56.8 %copy-start.9 = (s32[64]{0:T(128)S(1)}, s32[64]{0:T(128)}, u32[]{:S(2)}) copy-start(s32[64]{0:T(128)} %param.15) | copy-start | bytes 772
  29.6 67.4 %copy-start.5 = (f32[1,64,2,32]{1,3,2,0:T(8,128)S(1)}, f32[1,64,2,32]{1,3,2,0:T(8,128)}, u32[]{:S(2)}) copy-start(f32[1,64,2,32]{1,3,2,0:T(8,128)} %param.11) | copy-start | bytes 49156
  29.6 67.4 %copy-start.6 = (f32[1,64,2,32]{1,3,2,0:T(8,128)S(1)}, f32[1,64,2,32]{1,3,2,0:T(8,128)}, u32[]{:S(2)}) copy-start(f32[1,64,2,32]{1,3,2,0:T(8,128)} %param.13) | copy-start | bytes 49156
  29.6 67.3 %copy-start.7 = (f32[64,1,2,32]{0,3,2,1:T(8,128)S(1)}, f32[64,1,2,32]{0,3,2,1:T(8,128)}, u32[]{:S(2)}) copy-start(f32[64,1,2,32]{0,3,2,1:T(8,128)} %param.12) | copy-start | bytes 49156
  41.3 55.6 %all-reduce.9.cloned.1.call-start = ((), (), s32[]{:S(2)}) async-start(), calls=%async_computation.8 | async-start | bytes 262144
  42.1 127.4 %reduce-scatter.7.cloned.1.call-start = ((), (), s32[]{:S(2)}) async-start(), calls=%async_computation.5 | async-start | bytes 81920 | tf_op jit(solution)/shard_map/reduce_scatter | solution.py:89
  117.3 6.8 %copy-start.1 = (bf16[1,64,2,128,128]{4,3,2,1,0:T(8,128)(2,1)S(1)}, bf16[1,64,2,128,128]{4,3,2,1,0:T(8,128)(2,1)}, u32[]{:S(2)}) copy-start(bf16[1,64,2,128,128]{4,3,2,1,0:T(8,128)(2,1)} %param.9) | copy-start | bytes 12582916
  129.0 75.2 %all-reduce.11.cloned.1.call-start = ((), (), s32[]{:S(2)}) async-start(), calls=%async_computation.9 | async-start | bytes 262144
  169.5 107.4 %reduce-scatter.9.cloned.1.call-start = ((), (), s32[]{:S(2)}) async-start(), calls=%async_computation.6 | async-start | bytes 81920 | tf_op jit(solution)/shard_map/reduce_scatter | solution.py:89
  224.6 6.8 %copy-start.2 = (bf16[1,64,2,128,128]{4,3,2,1,0:T(8,128)(2,1)S(1)}, bf16[1,64,2,128,128]{4,3,2,1,0:T(8,128)(2,1)}, u32[]{:S(2)}) copy-start(bf16[1,64,2,128,128]{4,3,2,1,0:T(8,128)(2,1)} %param.9) | copy-start | bytes 12582916
  236.4 75.1 %all-reduce.13.cloned.1.call-start = ((), (), s32[]{:S(2)}) async-start(), calls=%async_computation.10 | async-start | bytes 262144
  276.8 107.2 %reduce-scatter.11.cloned.1.call-start = ((), (), s32[]{:S(2)}) async-start(), calls=%async_computation.7 | async-start | bytes 81920 | tf_op jit(solution)/shard_map/reduce_scatter | solution.py:89
  331.8 6.8 %copy-start.3 = (bf16[1,64,2,128,128]{4,3,2,1,0:T(8,128)(2,1)S(1)}, bf16[1,64,2,128,128]{4,3,2,1,0:T(8,128)(2,1)}, u32[]{:S(2)}) copy-start(bf16[1,64,2,128,128]{4,3,2,1,0:T(8,128)(2,1)} %param.9) | copy-start | bytes 12582916
  343.5 75.1 %all-reduce.15.cloned.1.call-start = ((), (), s32[]{:S(2)}) async-start(), calls=%async_computation.11 | async-start | bytes 262144
Sparse Core Ops, SparseCore 0:
  41.4 20.3 reduce-scatter.4
  64.2 32.6 all-reduce.8
  129.1 18.5 reduce-scatter.6
  169.6 34.5 all-reduce.10
  236.5 18.5 reduce-scatter.8
  276.9 34.5 all-reduce.12
  343.6 18.5 reduce-scatter.10
  384.1 34.5 all-reduce.14
where the time goes:
time: 438 us; the launch traced here: 437 us
  blocking collectives  244 us (56%)
  waiting for transfers between devices  111 us (25%)
  other arithmetic  51.5 us (12%)
  between operations  19.1 us (4%)
  local copies, waits for them, and re-layouts  10.6 us (2%)
    psum x4, blocking collectives, sweep_terms(): total = lax.psum(power, ('chan', 'srow', 'scol'))  158 us
    unnamed x12, waiting for transfers between devices  111 us
    all_gather x4, blocking collectives, shards(): g_row = lax.all_gather(g, 'scol', axis=2, tiled=True)  55.9 us
    reduce_sum x4, other arithmetic, local_terms(): pred_real = jnp.sum(r_real * z_real - r_imag * z_imag, axis=0)  24.7 us
    all_gather x4, blocking collectives, sweep_terms(): g_col = lax.all_gather(own_gains, 'srow', axis=2, tiled=True)  22 us
    reduce_sum x4, other arithmetic, local_terms(): cross_real = jnp.sum(z_real * w_real[None] + z_imag * w_imag[None], axis=-1)  16.5 us
  transfers between devices with their start and end apart: 8, of which 4 were waited for; matrix products, arithmetic and copies ran while one was open for 2% of the time, Pallas kernels for 0%

commit v1 on v0

--- a/solution.py
+++ b/solution.py
@@ -61,7 +61,7 @@
 def sweep_terms(vis_block, model_block, weight, g_row, own_gains, rho_dir, groups):
     g_col = lax.all_gather(own_gains, "srow", axis=2, tiled=True)
     power, a_term, cross = local_terms(vis_block, model_block, weight, g_row, g_col)
-    total = lax.psum(power, ("chan", "srow", "scol"))
+    total = lax.psum(lax.psum(power, ("srow", "scol")), "chan")
     rho_eff = rho_dir * (total / (groups * STATIONS * STATIONS) + EPS)
     return (a_term, cross, rho_eff)
 

time: 438 us -> 466 us (1.064)
  waiting for transfers between devices: 111 us -> 140 us
    reduce_scatter x4, waiting for transfers between devices: 0.08 us -> 27.9 us  [shards(): lax.psum_scatter(a_term[:, None, :], 'scol', scatter_dimension=2, tiled=T...]
    psum x4 -> x8, blocking collectives: 158 us -> 156 us  [sweep_terms(): total = lax.psum(lax.psum(power, ('srow', 'scol')), 'chan')]
  transfers between devices with their start and end apart: 8 -> 8, of which waited for: 4 -> 7; matrix products, arithmetic and copies ran while one was open for 2% -> 2% of each run, Pallas kernels for 0% -> 0%
where the time goes in v1:
time: 466 us; the launch traced here: 464 us
  blocking collectives  242 us (52%)
  waiting for transfers between devices  140 us (30%)
  other arithmetic  51.4 us (11%)
  between operations  19.1 us (4%)
  local copies, waits for them, and re-layouts  10.6 us (2%)
    psum x8, blocking collectives, sweep_terms(): total = lax.psum(lax.psum(power, ('srow', 'scol')), 'chan')  156 us
    unnamed x12, waiting for transfers between devices  112 us
    all_gather x4, blocking collectives, shards(): g_row = lax.all_gather(g, 'scol', axis=2, tiled=True)  55.9 us
    reduce_scatter x4, waiting for transfers between devices, shards(): lax.psum_scatter(a_term[:, None, :], 'scol', scatter_dimension=2, tiled=T...  27.9 us
    reduce_sum x4, other arithmetic, local_terms(): pred_real = jnp.sum(r_real * z_real - r_imag * z_imag, axis=0)  24.7 us
    all_gather x4, blocking collectives, sweep_terms(): g_col = lax.all_gather(own_gains, 'srow', axis=2, tiled=True)  22 us
    reduce_sum x4, other arithmetic, local_terms(): cross_real = jnp.sum(z_real * w_real[None] + z_imag * w_imag[None], axis=-1)  16.5 us
  transfers between devices with their start and end apart: 8, of which 7 were waited for; matrix products, arithmetic and copies ran while one was open for 2% of the time, Pallas kernels for 0%

profile of v1, /device:TPU:0, one launch (start us, length us, event | category | flops | bytes accessed | tf_op | source)
XLA Modules:
  0.0 464.3 jit_solution(11140758476280336848)
XLA Ops:
  7.2 15.3 %all-gather.1 = f32[1,64,2,128]{1,3,2,0:T(8,128)S(1)} all-gather(f32[1,64,2,32]{1,3,2,0:T(8,128)} %param.11), channel_id=3, replica_groups=mesh['chan'=2,'srow'=4,'scol'=4] {'scol'}, dimensions={3}, use_global_device_ids=true | all-gather | bytes 81920 | tf_op jit(solution)/shard_map/all_gather | solution.py:84
  22.5 5.6 %all-gather = f32[1,64,2,128]{1,3,2,0:T(8,128)S(1)} all-gather(f32[1,64,2,32]{1,3,2,0:T(8,128)} %param.11), channel_id=2, replica_groups=mesh['chan'=2,'srow'=4,'scol'=4] {'srow'}, dimensions={3}, use_global_device_ids=true | all-gather | bytes 81920 | tf_op jit(solution)/shard_map/all_gather | solution.py:62
  29.6 6.2 %subtract_reduce_fusion.7 = (f32[128,128]{1,0:T(8,128)S(1)}, f32[128,128]{1,0:T(8,128)S(1)}) fusion(f32[64,128]{1,0:T(8,128)S(1)} %copy.125, f32[64,128]{1,0:T(8,128)S(1)} %copy.124, f32[64,128]{1,0:T(8,128)S(1)} %copy.122, f32[64,128]{1,0:T(8,128)S(1)} %copy.121, bf16[64,2,128,128]{3,2,1,0:T(8,128)(2,1)} %bitcast.195), kind=kLoop, calls=%fused_computation.43 | loop fusion | flops 16744448 | bytes 4456448 | tf_op jit(solution)/shard_map/reduce_sum | solution.py:31
  36.4 4.1 add_reduce_fusion.6
  40.6 0.7 copy.130
  41.4 0.8 copy.128
  42.8 34.9 %psum.63 = f32[]{:T(128)} all-reduce(f32[]{:T(128)} %get-tuple-element.47), channel_id=1, replica_groups=mesh['chan'=2,'srow'=4,'scol'=4] {'srow','scol'}, use_global_device_ids=true, to_apply=%region_9.10 | all-reduce | flops 1 | bytes 8 | tf_op jit(solution)/shard_map/psum | solution.py:64
  79.0 5.6 %psum.64 = f32[]{:T(128)} all-reduce(f32[]{:T(128)} %psum.63), channel_id=1, replica_groups=mesh['chan'=2,'srow'=4,'scol'=4] {'chan'}, use_global_device_ids=true, to_apply=%region_10.11 | all-reduce | flops 1 | bytes 8 | tf_op jit(solution)/shard_map/psum | solution.py:64
  86.7 0.7 broadcast_add_fusion.3
  87.4 9.6 %all-reduce.9.cloned.1.call-done = f32[64,2,128]{0,1,2:T(2,128)} async-done(((f32[64,2,128]{0,1,2:T(2,128)}), f32[64,2,128]{0,1,2:T(2,128)}) %all-reduce.9.cloned.1.call-update) | async-done | bytes 65552
  97.0 0.9 bitcast_add_fusion.1
  97.9 13.5 %all_gather.27 = f32[64,2,128]{0,1,2:T(2,128)S(1)} all-gather(f32[64,2,32]{0,1,2:T(2,128)S(1)} %get-tuple-element.45), channel_id=1, replica_groups=mesh['chan'=2,'srow'=4,'scol'=4] {'scol'}, dimensions={2}, use_global_device_ids=true | all-gather | bytes 81920 | tf_op jit(solution)/shard_map/all_gather | solution.py:84
  111.4 5.4 %all_gather.26 = f32[64,2,128]{0,1,2:T(2,128)S(1)} all-gather(f32[64,2,32]{0,1,2:T(2,128)S(1)} %get-tuple-element.45), channel_id=1, replica_groups=mesh['chan'=2,'srow'=4,'scol'=4] {'srow'}, dimensions={2}, use_global_device_ids=true | all-gather | bytes 81920 | tf_op jit(solution)/shard_map/all_gather | solution.py:62
  117.4 6.2 %subtract_reduce_fusion.5 = (f32[128,128]{1,0:T(8,128)S(1)}, f32[128,128]{1,0:T(8,128)S(1)}) fusion(f32[64,128]{1,0:T(8,128)S(1)} %copy.136, f32[64,128]{1,0:T(8,128)S(1)} %copy.135, f32[64,128]{1,0:T(8,128)S(1)} %copy.134, f32[64,128]{1,0:T(8,128)S(1)} %copy.133, bf16[64,2,128,128]{3,2,1,0:T(8,128)(2,1)} %bitcast.196), kind=kLoop, calls=%fused_computation.38 | loop fusion | flops 16744448 | bytes 4456448 | tf_op jit(solution)/shard_map/reduce_sum | solution.py:31
  124.2 4.1 add_reduce_fusion.4
  128.3 0.7 copy.140
  129.0 33.0 %psum.65 = f32[]{:T(128)} all-reduce(f32[]{:T(128)} %get-tuple-element.42), channel_id=1, replica_groups=mesh['chan'=2,'srow'=4,'scol'=4] {'srow','scol'}, use_global_device_ids=true, to_apply=%region_19.20 | all-reduce | flops 1 | bytes 8 | tf_op jit(solution)/shard_map/psum | solution.py:64
  162.1 5.6 %psum.66 = f32[]{:T(128)} all-reduce(f32[]{:T(128)} %psum.65), channel_id=1, replica_groups=mesh['chan'=2,'srow'=4,'scol'=4] {'chan'}, use_global_device_ids=true, to_apply=%region_20.21 | all-reduce | flops 1 | bytes 8 | tf_op jit(solution)/shard_map/psum | solution.py:64
  168.4 0.8 copy.139
  169.2 9.3 %reduce-scatter.7.cloned.1.call-done = f32[64,1,32]{0,1,2:T(1,128)} async-done(((f32[64,1,128]{0,1,2:T(1,128)}), f32[64,1,32]{0,1,2:T(1,128)}) %reduce-scatter.7.cloned.1.call-update) | async-done | bytes 8208 | tf_op jit(solution)/shard_map/reduce_scatter | solution.py:89
  178.5 0.7 broadcast_add_fusion.2
  179.2 34.2 %all-reduce.11.cloned.1.call-done = f32[64,2,128]{0,1,2:T(2,128)} async-done(((f32[64,2,128]{0,1,2:T(2,128)}), f32[64,2,128]{0,1,2:T(2,128)}) %all-reduce.11.cloned.1.call-update) | async-done | bytes 65552
  213.4 0.8 multiply_add_fusion.2
  214.2 13.5 %all_gather.29 = f32[64,2,128]{0,1,2:T(2,128)S(1)} all-gather(f32[64,2,32]{0,1,2:T(2,128)S(1)} %multiply_add_fusion.2), channel_id=1, replica_groups=mesh['chan'=2,'srow'=4,'scol'=4] {'scol'}, dimensions={2}, use_global_device_ids=true | all-gather | bytes 81920 | tf_op jit(solution)/shard_map/all_gather | solution.py:84
  227.8 5.4 %all_gather.28 = f32[64,2,128]{0,1,2:T(2,128)S(1)} all-gather(f32[64,2,32]{0,1,2:T(2,128)S(1)} %multiply_add_fusion.2), channel_id=1, replica_groups=mesh['chan'=2,'srow'=4,'scol'=4] {'srow'}, dimensions={2}, use_global_device_ids=true | all-gather | bytes 81920 | tf_op jit(solution)/shard_map/all_gather | solution.py:62
  233.7 6.2 %subtract_reduce_fusion.3 = (f32[128,128]{1,0:T(8,128)S(1)}, f32[128,128]{1,0:T(8,128)S(1)}) fusion(f32[64,128]{1,0:T(8,128)S(1)} %copy.144, f32[64,128]{1,0:T(8,128)S(1)} %copy.143, f32[64,128]{1,0:T(8,128)S(1)} %copy.142, f32[64,128]{1,0:T(8,128)S(1)} %copy.141, bf16[64,2,128,128]{3,2,1,0:T(8,128)(2,1)} %bitcast.197), kind=kLoop, calls=%fused_computation.33 | loop fusion | flops 16744448 | bytes 4456448 | tf_op jit(solution)/shard_map/reduce_sum | solution.py:31
  240.5 4.1 add_reduce_fusion.2
  244.7 0.7 copy.148
  245.4 33.0 %psum.67 = f32[]{:T(128)} all-reduce(f32[]{:T(128)} %get-tuple-element.39), channel_id=1, replica_groups=mesh['chan'=2,'srow'=4,'scol'=4] {'srow','scol'}, use_global_device_ids=true, to_apply=%region_29.30 | all-reduce | flops 1 | bytes 8 | tf_op jit(solution)/shard_map/psum | solution.py:64
  278.5 5.6 %psum.68 = f32[]{:T(128)} all-reduce(f32[]{:T(128)} %psum.67), channel_id=1, replica_groups=mesh['chan'=2,'srow'=4,'scol'=4] {'chan'}, use_global_device_ids=true, to_apply=%region_30.31 | all-reduce | flops 1 | bytes 8 | tf_op jit(solution)/shard_map/psum | solution.py:64
  284.7 0.8 copy.147
  285.6 9.3 %reduce-scatter.9.cloned.1.call-done = f32[64,1,32]{0,1,2:T(1,128)} async-done(((f32[64,1,128]{0,1,2:T(1,128)}), f32[64,1,32]{0,1,2:T(1,128)}) %reduce-scatter.9.cloned.1.call-update) | async-done | bytes 8208 | tf_op jit(solution)/shard_map/reduce_scatter | solution.py:89
  294.9 0.7 broadcast_add_fusion.1
  295.6 34.2 %all-reduce.13.cloned.1.call-done = f32[64,2,128]{0,1,2:T(2,128)} async-done(((f32[64,2,128]{0,1,2:T(2,128)}), f32[64,2,128]{0,1,2:T(2,128)}) %all-reduce.13.cloned.1.call-update) | async-done | bytes 65552
  329.8 0.8 multiply_add_fusion.1
  330.6 13.5 %all_gather.31 = f32[64,2,128]{0,1,2:T(2,128)S(1)} all-gather(f32[64,2,32]{0,1,2:T(2,128)S(1)} %multiply_add_fusion.1), channel_id=1, replica_groups=mesh['chan'=2,'srow'=4,'scol'=4] {'scol'}, dimensions={2}, use_global_device_ids=true | all-gather | bytes 81920 | tf_op jit(solution)/shard_map/all_gather | solution.py:84
  344.1 5.6 %all_gather.30 = f32[64,2,128]{0,1,2:T(2,128)S(1)} all-gather(f32[64,2,32]{0,1,2:T(2,128)S(1)} %multiply_add_fusion.1), channel_id=1, replica_groups=mesh['chan'=2,'srow'=4,'scol'=4] {'srow'}, dimensions={2}, use_global_device_ids=true | all-gather | bytes 81920 | tf_op jit(solution)/shard_map/all_gather | solution.py:62
  350.3 6.2 %subtract_reduce_fusion.1 = (f32[128,128]{1,0:T(8,128)S(1)}, f32[128,128]{1,0:T(8,128)S(1)}) fusion(f32[64,128]{1,0:T(8,128)S(1)} %copy.152, f32[64,128]{1,0:T(8,128)S(1)} %copy.151, f32[64,128]{1,0:T(8,128)S(1)} %copy.150, f32[64,128]{1,0:T(8,128)S(1)} %copy.149, bf16[64,2,128,128]{3,2,1,0:T(8,128)(2,1)} %bitcast.198), kind=kLoop, calls=%fused_computation.28 | loop fusion | flops 16744448 | bytes 4456448 | tf_op jit(solution)/shard_map/reduce_sum | solution.py:31
  357.1 4.1 add_reduce_fusion
  361.2 0.7 copy.156
  361.9 33.0 %psum.69 = f32[]{:T(128)} all-reduce(f32[]{:T(128)} %get-tuple-element.36), channel_id=1, replica_groups=mesh['chan'=2,'srow'=4,'scol'=4] {'srow','scol'}, use_global_device_ids=true, to_apply=%region_39.40 | all-reduce | flops 1 | bytes 8 | tf_op jit(solution)/shard_map/psum | solution.py:64
  395.0 5.6 %psum.70 = f32[]{:T(128)} all-reduce(f32[]{:T(128)} %psum.69), channel_id=1, replica_groups=mesh['chan'=2,'srow'=4,'scol'=4] {'chan'}, use_global_device_ids=true, to_apply=%region_40.41 | all-reduce | flops 1 | bytes 8 | tf_op jit(solution)/shard_map/psum | solution.py:64
  401.3 0.8 copy.155
  402.1 9.3 %reduce-scatter.11.cloned.1.call-done = f32[64,1,32]{0,1,2:T(1,128)} async-done(((f32[64,1,128]{0,1,2:T(1,128)}), f32[64,1,32]{0,1,2:T(1,128)}) %reduce-scatter.11.cloned.1.call-update) | async-done | bytes 8208 | tf_op jit(solution)/shard_map/reduce_scatter | solution.py:89
  411.4 0.7 broadcast_add_fusion
  412.1 34.3 %all-reduce.15.cloned.1.call-done = f32[64,2,128]{0,1,2:T(2,128)} async-done(((f32[64,2,128]{0,1,2:T(2,128)}), f32[64,2,128]{0,1,2:T(2,128)}) %all-reduce.15.cloned.1.call-update) | async-done | bytes 65552
  446.5 0.8 fusion.21
  447.9 8.3 %psum.71 = f32[64,1,2,32]{0,2,3,1:T(2,128)S(1)} all-reduce(f32[64,1,2,32]{0,2,3,1:T(2,128)S(1)} %get-tuple-element.34), channel_id=1, replica_groups=mesh['chan'=2,'srow'=4,'scol'=4] {'chan'}, use_global_device_ids=true, to_apply=%region_41.42 | all-reduce | flops 4096 | bytes 32768 | tf_op jit(solution)/shard_map/psum | solution.py:94
  (88 shorter events, 9.2 us)
Async XLA Ops:
  7.2 28.6 %copy-start.4 = (bf16[1,2,128,128]{3,2,1,0:T(8,128)(2,1)S(1)}, bf16[1,2,128,128]{3,2,1,0:T(8,128)(2,1)}, u32[]{:S(2)}) copy-start(bf16[1,2,128,128]{3,2,1,0:T(8,128)(2,1)} %param.8) | copy-start | bytes 196612
  7.2 79.5 %reduce-scatter.5.cloned.1.call-start = ((), (), s32[]{:S(2)}) async-start(), calls=%async_computation.4 | async-start | bytes 81920 | tf_op jit(solution)/shard_map/reduce_scatter | solution.py:89
  29.5 6.9 %copy-start = (bf16[1,64,2,128,128]{4,3,2,1,0:T(8,128)(2,1)S(1)}, bf16[1,64,2,128,128]{4,3,2,1,0:T(8,128)(2,1)}, u32[]{:S(2)}) copy-start(bf16[1,64,2,128,128]{4,3,2,1,0:T(8,128)(2,1)} %param.9) | copy-start | bytes 12582916
  29.5 48.2 %copy-start.10 = (u32[32]{0:T(128)S(1)}, u32[32]{0:T(128)}, u32[]{:S(2)}) copy-start(u32[32]{0:T(128)} %constant.53) | copy-start | bytes 388
  29.5 56.4 %copy-start.8 = (f32[8]{0:T(128)S(1)}, f32[8]{0:T(128)}, u32[]{:S(2)}) copy-start(f32[8]{0:T(128)} %param.14) | copy-start | bytes 100
  29.5 56.4 %copy-start.9 = (s32[64]{0:T(128)S(1)}, s32[64]{0:T(128)}, u32[]{:S(2)}) copy-start(s32[64]{0:T(128)} %param.15) | copy-start | bytes 772
  29.6 67.4 %copy-start.5 = (f32[1,64,2,32]{1,3,2,0:T(8,128)S(1)}, f32[1,64,2,32]{1,3,2,0:T(8,128)}, u32[]{:S(2)}) copy-start(f32[1,64,2,32]{1,3,2,0:T(8,128)} %param.11) | copy-start | bytes 49156
  29.6 67.4 %copy-start.6 = (f32[1,64,2,32]{1,3,2,0:T(8,128)S(1)}, f32[1,64,2,32]{1,3,2,0:T(8,128)}, u32[]{:S(2)}) copy-start(f32[1,64,2,32]{1,3,2,0:T(8,128)} %param.13) | copy-start | bytes 49156
  29.6 67.4 %copy-start.7 = (f32[64,1,2,32]{0,3,2,1:T(8,128)S(1)}, f32[64,1,2,32]{0,3,2,1:T(8,128)}, u32[]{:S(2)}) copy-start(f32[64,1,2,32]{0,3,2,1:T(8,128)} %param.12) | copy-start | bytes 49156
  41.3 55.7 %all-reduce.9.cloned.1.call-start = ((), (), s32[]{:S(2)}) async-start(), calls=%async_computation.8 | async-start | bytes 262144
  42.1 136.4 %reduce-scatter.7.cloned.1.call-start = ((), (), s32[]{:S(2)}) async-start(), calls=%async_computation.5 | async-start | bytes 81920 | tf_op jit(solution)/shard_map/reduce_scatter | solution.py:89
  117.3 6.8 %copy-start.1 = (bf16[1,64,2,128,128]{4,3,2,1,0:T(8,128)(2,1)S(1)}, bf16[1,64,2,128,128]{4,3,2,1,0:T(8,128)(2,1)}, u32[]{:S(2)}) copy-start(bf16[1,64,2,128,128]{4,3,2,1,0:T(8,128)(2,1)} %param.9) | copy-start | bytes 12582916
  162.1 51.3 %all-reduce.11.cloned.1.call-start = ((), (), s32[]{:S(2)}) async-start(), calls=%async_computation.9 | async-start | bytes 262144
  169.2 125.7 %reduce-scatter.9.cloned.1.call-start = ((), (), s32[]{:S(2)}) async-start(), calls=%async_computation.6 | async-start | bytes 81920 | tf_op jit(solution)/shard_map/reduce_scatter | solution.py:89
  233.7 6.8 %copy-start.2 = (bf16[1,64,2,128,128]{4,3,2,1,0:T(8,128)(2,1)S(1)}, bf16[1,64,2,128,128]{4,3,2,1,0:T(8,128)(2,1)}, u32[]{:S(2)}) copy-start(bf16[1,64,2,128,128]{4,3,2,1,0:T(8,128)(2,1)} %param.9) | copy-start | bytes 12582916
  278.4 51.3 %all-reduce.13.cloned.1.call-start = ((), (), s32[]{:S(2)}) async-start(), calls=%async_computation.10 | async-start | bytes 262144
  285.5 125.9 %reduce-scatter.11.cloned.1.call-start = ((), (), s32[]{:S(2)}) async-start(), calls=%async_computation.7 | async-start | bytes 81920 | tf_op jit(solution)/shard_map/reduce_scatter | solution.py:89
  350.3 6.8 %copy-start.3 = (bf16[1,64,2,128,128]{4,3,2,1,0:T(8,128)(2,1)S(1)}, bf16[1,64,2,128,128]{4,3,2,1,0:T(8,128)(2,1)}, u32[]{:S(2)}) copy-start(bf16[1,64,2,128,128]{4,3,2,1,0:T(8,128)(2,1)} %param.9) | copy-start | bytes 12582916
  395.0 51.5 %all-reduce.15.cloned.1.call-start = ((), (), s32[]{:S(2)}) async-start(), calls=%async_computation.11 | async-start | bytes 262144
Sparse Core Ops, SparseCore 0:
  41.4 20.3 reduce-scatter.4
  64.2 32.7 all-reduce.8
  162.2 16.2 reduce-scatter.6
  180.8 32.5 all-reduce.10
  278.6 16.2 reduce-scatter.8
  297.1 32.5 all-reduce.12
  395.1 16.2 reduce-scatter.10
  413.8 32.5 all-reduce.14
